TPU v7x, 128 devices: a whole 4x4x4 slice. The times are simulated.
128 devices in a mesh: proj: 16 (over z_lo, y, core), row: 8 (over x, z_hi).
Axes of the slice: x: 4, y: 4, z: 4 (z_hi: 2, z_lo: 2; z = z_hi * 2 + z_lo), core: 2. Of those that a mesh axis runs over, the one named last changes fastest.
Arguments:
- projections: float32 [8192, 8, 1536], P('proj', 'row'), may hold values from -40000 to 40000
Outputs:
- gram: float32 [8192, 8192], P('proj', 'row')
All inputs are finite; a program needn't handle non-finite values.
Results may differ from a plain program's by a relative error of at most 0.0017.
Values may be sent and summed in bfloat16 or wider, within the bound.
A program may use at most 128 MiB of HBM per device.

v0:
```python
import math
import jax
import jax.numpy as jnp
from jax import lax
from jax.sharding import PartitionSpec as P


def per_device(projections):
    tile_rows, det_rows, columns = projections.shape
    entries = det_rows * lax.axis_size("row") * columns
    filtered = projections - jnp.mean(projections, axis=2, keepdims=True)
    energy = lax.psum(jnp.sum(filtered * filtered, axis=(1, 2)), "row")
    band_power = energy / entries
    normed = (
        filtered * lax.rsqrt(band_power + 1e-05)[:, None, None] * (1.0 / math.sqrt(entries))
    ).astype(jnp.bfloat16)
    flattened = normed.reshape(tile_rows, det_rows * columns)
    contract = (((1,), (1,)), ((), ()))
    product = lax.dot_general(
        flattened,
        lax.all_gather(flattened, "proj", axis=0, tiled=True),
        contract,
        preferred_element_type=jnp.float32,
    )
    return lax.psum_scatter(product, "row", scatter_dimension=1, tiled=True)


def solution(mesh):
    in_specs = (P("proj", "row", None),)
    out_specs = P("proj", "row")
    return jax.shard_map(
        per_device, mesh=mesh, in_specs=in_specs, out_specs=out_specs, check_vma=False
    )
```

profile of v0, /device:TPU:0, one launch (start us, length us, event | category | flops | bytes accessed | tf_op | source)
XLA Modules:
  0.0 388.9 jit_solution(17753626626749477230)
XLA Ops:
  6.5 0.0 copy-start
  6.5 0.0 all-gather.3.cloned.1.call-start
  6.5 4.2 %reduce_sum.18 = f32[512]{0:T(512)S(1)} reduce(f32[512,1,1536]{2,1,0:T(1,128)} %param.1, f32[]{:T(128)} %constant.2.clone.1), dimensions={1,2}, to_apply=%region_0.0 | reduce | flops 785920 | bytes 3147780 | tf_op jit(solution)/shard_map/reduce_sum | solution.py:11
  10.8 0.0 copy-done
  10.8 0.4 multiply_reduce_fusion
  11.3 25.1 %psum.7 = f32[512]{0:T(512)S(1)} all-reduce(f32[512]{0:T(512)S(1)} %multiply_reduce_fusion), channel_id=1, replica_groups=mesh['proj'=16,'row'=8] {'row'}, use_global_device_ids=true, to_apply=%region_2.0 | all-reduce | flops 512 | bytes 4096 | tf_op jit(solution)/shard_map/psum | solution.py:12
  36.4 1.6 multiply_convert_fusion
  38.0 0.0 all-gather.3.cloned.1.call-update
  38.0 0.0 reduce-scatter.2.cloned.1.call-start
  38.1 128.1 %all-gather.3.cloned.1.call-done = bf16[8192,1,1536]{2,0,1:T(8,128)(2,1)} async-done(((bf16[512,1,1536]{2,0,1:T(8,128)(2,1)}), bf16[8192,1,1536]{2,0,1:T(8,128)(2,1)}) %all-gather.3.cloned.1.call-update) | async-done | bytes 25165840 | tf_op jit(solution)/shard_map/all_gather | solution.py:21
  166.2 20.8 %fusion = f32[512,8192]{1,0:T(8,128)} fusion(bf16[8192,1,1536]{2,0,1:T(8,128)(2,1)} %all-gather.3.cloned.1.call-done, bf16[512,1,1536]{2,0,1:T(8,128)(2,1)} %multiply_convert_fusion), kind=kOutput, calls=%fused_computation | convolution fusion | flops 12884901888 | bytes 43515904 | tf_op jit(solution)/shard_map/dot_general | solution.py:19
  187.0 0.0 reduce-scatter.2.cloned.1.call-update
  187.1 195.0 %reduce-scatter.2.cloned.1.call-done = f32[512,1024]{1,0:T(8,128)} async-done(((f32[512,8192]{1,0:T(8,128)}), f32[512,1024]{1,0:T(8,128)}) %reduce-scatter.2.cloned.1.call-update) | async-done | bytes 2097168 | tf_op jit(solution)/shard_map/reduce_scatter | solution.py:25
  (2 shorter events, 0.0 us)
Async XLA Ops:
  6.5 4.3 %copy-start = (f32[512,1,1536]{2,1,0:T(1,128)S(1)}, f32[512,1,1536]{2,1,0:T(1,128)}, u32[]{:S(2)}) copy-start(f32[512,1,1536]{2,1,0:T(1,128)} %param.1) | copy-start | bytes 9437188
  6.5 159.7 %all-gather.3.cloned.1.call-start = ((), (), s32[]{:S(2)}) async-start(), calls=%async_computation.2 | async-start | bytes 26738688 | tf_op jit(solution)/shard_map/all_gather | solution.py:21
  38.0 344.1 %reduce-scatter.2.cloned.1.call-start = ((), (), s32[]{:S(2)}) async-start(), calls=%async_computation.1 | async-start | bytes 18874368 | tf_op jit(solution)/shard_map/reduce_scatter | solution.py:25
Sparse Core Ops, SparseCore 0:
  38.2 127.9 all-gather.2
  187.2 194.8 reduce-scatter.1
where the time goes:
time: 389 us
  waiting for transfers between devices  323 us (83%)
  blocking collectives  25.1 us (6%)
  matrix products  20.8 us (5%)
  between operations  13.4 us (3%)
  other arithmetic  6.33 us (2%)
    reduce_scatter x1, waiting for transfers between devices, per_device(): return lax.psum_scatter(product, 'row', scatter_dimension=1, tiled=True)  195 us
    all_gather x1, waiting for transfers between devices, per_device(): lax.all_gather(flattened, 'proj', axis=0, tiled=True)  128 us
    psum x1, blocking collectives, per_device(): energy = lax.psum(jnp.sum(filtered * filtered, axis=(1, 2)), 'row')  25.1 us
    dot_general x1, matrix products, per_device(): lax.dot_general(flattened, lax.all_gather(flattened, 'proj', axis=0, tile...  20.8 us
  transfers between devices with their start and end apart: 2, of which 2 were waited for; matrix products, arithmetic and copies ran while one was open for 0% of the time, Pallas kernels for 0%

commit v1 on v0

--- a/solution.py
+++ b/solution.py
@@ -18,7 +18,9 @@
     contract = (((1,), (1,)), ((), ()))
     product = lax.dot_general(
         flattened,
-        lax.all_gather(flattened, "proj", axis=0, tiled=True),
+        jnp.concatenate(
+            lax.all_to_all(jnp.stack([flattened] * lax.axis_size("proj")), "proj", 0, 0), axis=0
+        ),
         contract,
         preferred_element_type=jnp.float32,
     )

time: 389 us -> 543 us (1.40)
  blocking collectives: 25.1 us -> 305 us
  waiting for transfers between devices: 323 us -> 188 us
  other arithmetic: 6.33 us -> 12.9 us
    all_to_all x0 -> x1, blocking collectives: none -> 280 us  [per_device(): lax.all_to_all(jnp.stack([flattened] * lax.axis_size('proj')), 'proj', 0, 0)]
    all_gather x1 -> x0, waiting for transfers between devices: 128 us -> none  [per_device(): lax.all_gather(flattened, 'proj', axis=0, tiled=True)]
    reduce_scatter x1, waiting for transfers between devices: 195 us -> 188 us  [per_device(): return lax.psum_scatter(product, 'row', scatter_dimension=1, tiled=True)]
  transfers between devices with their start and end apart: 2 -> 1, of which waited for: 2 -> 1; matrix products, arithmetic and copies ran while one was open for 0% -> 0% of each run, Pallas kernels for 0% -> 0%
where the time goes in v1:
time: 543 us
  blocking collectives  305 us (56%)
  waiting for transfers between devices  188 us (35%)
  matrix products  20.4 us (4%)
  between operations  13.4 us (2%)
  other arithmetic  12.9 us (2%)
    all_to_all x1, blocking collectives, per_device(): lax.all_to_all(jnp.stack([flattened] * lax.axis_size('proj')), 'proj', 0, 0)  280 us
    reduce_scatter x1, waiting for transfers between devices, per_device(): return lax.psum_scatter(product, 'row', scatter_dimension=1, tiled=True)  188 us
    psum x1, blocking collectives, per_device(): energy = lax.psum(jnp.sum(filtered * filtered, axis=(1, 2)), 'row')  25.1 us
    dot_general x1, matrix products, per_device(): lax.dot_general(flattened, jnp.concatenate(lax.all_to_all(jnp.stack([flat...  20.4 us
  transfers between devices with their start and end apart: 1, of which 1 were waited for; matrix products, arithmetic and copies ran while one was open for 0% of the time, Pallas kernels for 0%

profile of v1, /device:TPU:0, one launch (start us, length us, event | category | flops | bytes accessed | tf_op | source)
XLA Modules:
  0.0 542.8 jit_solution(8581784884207246084)
XLA Ops:
  6.5 0.0 copy-start
  6.5 0.0 reduce-scatter.2.cloned.1.call-start
  6.5 4.2 reduce_sum.18
  10.8 0.0 copy-done
  10.8 3.9 multiply_reduce_fusion
  14.7 25.1 %psum.7 = f32[512]{0:T(512)S(1)} all-reduce(f32[512]{0:T(512)S(1)} %multiply_reduce_fusion), channel_id=1, replica_groups=mesh['proj'=16,'row'=8] {'row'}, use_global_device_ids=true, to_apply=%region_2.0 | all-reduce | flops 512 | bytes 4096 | tf_op jit(solution)/shard_map/psum | solution.py:12
  39.9 4.7 multiply_convert_fusion
  44.6 0.3 copy.4
  44.9 2.6 stack.3
  47.5 279.8 %all_to_all.5 = bf16[16,512,1536]{2,1,0:T(8,128)(2,1)} all-to-all(bf16[16,512,1536]{2,1,0:T(8,128)(2,1)S(1)} %stack.3), channel_id=1, replica_groups=mesh['proj'=16,'row'=8] {'proj'}, dimensions={0} | all-to-all | bytes 50331648 | tf_op jit(solution)/shard_map/all_to_all | solution.py:22
  327.3 20.4 %fusion = f32[512,8192]{1,0:T(8,128)} fusion(bf16[512,1536]{1,0:T(8,128)(2,1)S(1)} %bitcast.8, bf16[8192,1536]{1,0:T(8,128)(2,1)} %bitcast.6), kind=kOutput, calls=%fused_computation.5 | convolution fusion | flops 12884901888 | bytes 43515904 | tf_op jit(solution)/shard_map/dot_general | solution.py:19
  347.7 0.0 reduce-scatter.2.cloned.1.call-update
  347.7 188.3 %reduce-scatter.2.cloned.1.call-done = f32[512,1024]{1,0:T(8,128)} async-done(((f32[512,8192]{1,0:T(8,128)}), f32[512,1024]{1,0:T(8,128)}) %reduce-scatter.2.cloned.1.call-update) | async-done | bytes 2097168 | tf_op jit(solution)/shard_map/reduce_scatter | solution.py:27
  (2 shorter events, 0.0 us)
Async XLA Ops:
  6.5 4.3 copy-start
  6.5 529.4 %reduce-scatter.2.cloned.1.call-start = ((), (), s32[]{:S(2)}) async-start(), calls=%async_computation.2 | async-start | bytes 18874368 | tf_op jit(solution)/shard_map/reduce_scatter | solution.py:27
Sparse Core Ops, SparseCore 0:
  347.8 188.0 reduce-scatter.1
